TPU v7x, 32 devices: a whole 2x2x4 slice. The times are simulated.
32 devices in a mesh: leaf: 4 (over z), row: 2 (over y), col: 4 (over x, core).
Axes of the slice: x: 2, y: 2, z: 4, core: 2. Of those that a mesh axis runs over, the one named last changes fastest.
Arguments:
- rhs_root: bfloat16 [64, 4, 768], P('col', None, ('leaf', 'row')), may hold values from -6 to 6
- rhs_child: bfloat16 [64, 4, 768], P('col', None, ('leaf', 'row')), may hold values from -6 to 6
- subtree_update: bfloat16 [64, 4, 1024], P('col', None, ('leaf', 'row')), may hold values from -6 to 6
- inv_root: bfloat16 [4, 768, 3072], P(None, ('leaf', 'row'), 'col'), as said below
- inv_child: bfloat16 [4, 768, 1536], P(None, ('leaf', 'row'), 'col'), as said below
- off_child: bfloat16 [4, 1024, 1536], P(None, ('leaf', 'row'), 'col'), may hold values from -0.15625 to 0.15625
- child_map: int32 [2, 16], replicated, may hold values from 0 to 23, as said below
- subtree_map: int32 [4, 8], replicated, may hold values from 0 to 27, as said below
Outputs:
- solution_root: float32 [64, 4, 768], P('col', None, ('leaf', 'row'))
- solution_child: float32 [64, 4, 768], P('col', None, ('leaf', 'row'))
- leaf_solution: bfloat16 [64, 4, 1024], P('col', None, ('leaf', 'row'))
Inputs may be any that keep to these rules, and one draw needn't show every extreme that they name: `child_map`: each row names 16 different blocks. `subtree_map`: each row names 8 different blocks. `inv_root`: zero above the diagonal, positive on it. `inv_child`: each child's block is zero above the diagonal, positive on it.
All inputs are finite; a program needn't handle non-finite values.
Results may differ from a plain program's by a relative error of at most 0.017.
Values may be sent and summed in bfloat16 or wider, within the bound.
A program may use at most 64 MiB of HBM per device.

v0:
```python
import jax
import jax.numpy as jnp
from jax import lax
from jax.sharding import PartitionSpec as P

BLOCK_ROWS = 128


def partner_2(block, axis, bit):
    count = lax.axis_size(axis)
    route = []
    for low in range(count):
        high = low | 1 << bit
        if high != low and high < count:
            route += [(low, high), (high, low)]
    return lax.ppermute(block, axis, route)


def group_gather(piece, group_size):
    merged = lax.all_gather(piece, "row", axis=2, tiled=True)
    leaf_index = lax.axis_index("leaf")
    for bit_number in range(group_size.bit_length() - 1):
        partner = partner_2(merged, "leaf", bit_number)
        upper = leaf_index >> bit_number & 1 == 1
        merged = jnp.where(
            upper, jnp.concatenate([partner, merged], 2), jnp.concatenate([merged, partner], 2)
        )
    return merged


def group_sum(partial_sum, group_size):
    leaf_index = lax.axis_index("leaf")
    for bit_number in reversed(range(group_size.bit_length() - 1)):
        middle = partial_sum.shape[1] // 2
        lower_half = partial_sum[:, :middle]
        upper_half = partial_sum[:, middle:]
        upper = leaf_index >> bit_number & 1 == 1
        outgoing = jnp.where(upper, lower_half, upper_half)
        kept_half = jnp.where(upper, upper_half, lower_half)
        partial_sum = kept_half + partner_2(
            outgoing.astype(jnp.bfloat16), "leaf", bit_number
        ).astype(outgoing.dtype)
    return lax.psum_scatter(
        partial_sum.astype(jnp.bfloat16), "row", scatter_dimension=1, tiled=True
    ).astype(jnp.float32)


def one_hot(block_map, blocks_total):
    return (block_map[..., None] == jnp.arange(blocks_total, dtype=jnp.int32)).astype(jnp.bfloat16)


def pick_piece(source, position, along):
    return lax.dynamic_index_in_dim(source, position, along, keepdims=False)


def contract(left_side, right_side, left_dim, right_dim):
    return lax.dot_general(
        left_side,
        right_side,
        (((left_dim,), (right_dim,)), ((), ())),
        preferred_element_type=jnp.float32,
    )


def local(
    rhs_root, rhs_child, subtree_update, inv_root, inv_child, off_child, child_map, subtree_map
):
    n_col = lax.axis_size("col")
    n_row = lax.axis_size("row")
    n_leaf = lax.axis_size("leaf")
    group_size = n_leaf // 2
    sub_size = n_leaf // 4
    col_index = lax.axis_index("col")
    leaf_index = lax.axis_index("leaf")
    row_index = lax.axis_index("row")
    front_index = leaf_index // group_size
    member = leaf_index % group_size
    child_rank = member * n_row + row_index
    half_index = member // sub_size
    sub_rank = member % sub_size * n_row + row_index
    panel_width = rhs_child.shape[0]
    right_sides = panel_width * n_col
    sep_piece = rhs_child.shape[2]
    upd_piece = subtree_update.shape[2]
    root_width = inv_root.shape[2]
    child_width = inv_child.shape[2]
    child_order = child_width * n_col
    child_update = upd_piece * n_col * group_size * n_row
    root_blocks = root_width * n_col // BLOCK_ROWS
    child_blocks = (child_order + child_update) // BLOCK_ROWS
    root_matrix = inv_root.reshape(n_col * sep_piece, root_width)
    child_matrix = inv_child.reshape(n_col * sep_piece, child_width)
    off_matrix = off_child.reshape(n_col * upd_piece, child_width)
    joined = jnp.concatenate([subtree_update, rhs_child], 2)
    gathered = group_gather(joined, group_size).reshape(
        panel_width, n_col, group_size * n_row, upd_piece + sep_piece
    )
    sub_vectors = (
        gathered[..., :upd_piece]
        .reshape(panel_width, n_col, 2, -1)
        .transpose(2, 0, 1, 3)
        .reshape(2, panel_width, -1, BLOCK_ROWS)
    )
    child_rhs_full = gathered[..., upd_piece:].reshape(panel_width, child_order)
    sub_rows = lax.dynamic_slice_in_dim(subtree_map, 2 * front_index, 2, 0)
    spread = jnp.einsum(
        "hpjt,hjn->pnt",
        sub_vectors,
        one_hot(sub_rows, child_blocks),
        preferred_element_type=jnp.float32,
    ).reshape(panel_width, -1)
    child_sep = (spread[:, :child_order] + child_rhs_full.astype(jnp.float32)).astype(jnp.bfloat16)
    child_tail = spread[:, child_order:]
    child_tile = lax.all_to_all(
        child_sep.reshape(panel_width, n_col, child_width),
        "col",
        split_axis=1,
        concat_axis=0,
        tiled=True,
    ).reshape(right_sides, child_width)
    child_forward = lax.psum(contract(child_tile, child_matrix, 1, 1), "col").astype(jnp.bfloat16)
    forward_quarter = lax.dynamic_slice_in_dim(
        child_forward.reshape(right_sides, n_col, sep_piece), col_index, 1, 1
    )
    forward_tile = group_gather(forward_quarter, group_size).reshape(right_sides, child_width)
    pass_term = lax.psum_scatter(
        contract(forward_tile, off_matrix, 1, 1), "col", scatter_dimension=0, tiled=True
    )
    tail_mine = pick_piece(
        child_tail.reshape(panel_width, n_col, group_size * n_row, upd_piece), child_rank, 2
    )
    child_pass = (tail_mine - pass_term.reshape(panel_width, n_col, upd_piece)).astype(jnp.bfloat16)
    joined_root = jnp.concatenate([child_pass, rhs_root], 2)
    root_all = lax.all_gather(joined_root, ("leaf", "row"), axis=2, tiled=True).reshape(
        panel_width, n_col, n_leaf * n_row, upd_piece + sep_piece
    )
    pass_vectors = (
        root_all[..., :upd_piece]
        .reshape(panel_width, n_col, 2, -1)
        .transpose(2, 0, 1, 3)
        .reshape(2, panel_width, -1, BLOCK_ROWS)
    )
    root_rhs_full = root_all[..., upd_piece:].reshape(panel_width, root_width * n_col)
    root_spread = jnp.einsum(
        "hpjt,hjn->pnt",
        pass_vectors,
        one_hot(child_map, root_blocks),
        preferred_element_type=jnp.float32,
    ).reshape(panel_width, -1)
    root_sep = (root_spread + root_rhs_full.astype(jnp.float32)).astype(jnp.bfloat16)
    root_tile = lax.all_to_all(
        root_sep.reshape(panel_width, n_col, root_width),
        "col",
        split_axis=1,
        concat_axis=0,
        tiled=True,
    ).reshape(right_sides, root_width)
    root_forward = lax.psum(contract(root_tile, root_matrix, 1, 1), "col").astype(jnp.bfloat16)
    map_row = pick_piece(child_map, front_index, 0)
    root_piece = lax.psum_scatter(
        contract(root_matrix, root_forward, 0, 1), ("leaf", "row"), scatter_dimension=0, tiled=True
    )
    solution_root = lax.all_to_all(
        root_piece.T.reshape(right_sides, 1, sep_piece),
        "col",
        split_axis=0,
        concat_axis=1,
        tiled=True,
    )
    root_everywhere = lax.all_gather(
        solution_root.astype(jnp.bfloat16), ("leaf", "row"), axis=2, tiled=True
    ).reshape(panel_width, root_blocks, BLOCK_ROWS)
    known_full = (
        jnp.einsum(
            "pnt,jn->pjt",
            root_everywhere,
            one_hot(map_row, root_blocks),
            preferred_element_type=jnp.float32,
        )
        .astype(jnp.bfloat16)
        .reshape(panel_width, child_update)
    )
    known_mine = pick_piece(
        known_full.reshape(panel_width, n_col, group_size * n_row, upd_piece), child_rank, 2
    )
    known_rows = lax.all_gather(known_mine, "col", axis=0, tiled=True).reshape(
        right_sides, n_col * upd_piece
    )
    correction = group_sum(contract(known_rows, off_matrix, 1, 0), group_size)
    back_quarter = (
        forward_quarter.reshape(right_sides, sep_piece).astype(jnp.float32) - correction
    ).astype(jnp.bfloat16)
    back_rows = lax.all_gather(
        back_quarter.reshape(right_sides, 1, sep_piece), "col", axis=1, tiled=True
    ).reshape(right_sides, n_col * sep_piece)
    child_piece = group_sum(contract(back_rows, child_matrix, 1, 0), group_size)
    solution_child = lax.all_to_all(
        child_piece.reshape(right_sides, 1, sep_piece),
        "col",
        split_axis=0,
        concat_axis=1,
        tiled=True,
    )
    child_rounded = solution_child.astype(jnp.bfloat16)
    sep_whole = group_gather(child_rounded, group_size).reshape(panel_width, child_order)
    child_whole = jnp.concatenate([sep_whole, known_full], 1)
    sub_row = pick_piece(subtree_map, 2 * front_index + half_index, 0)
    leaf_full = jnp.einsum(
        "pnt,jn->pjt",
        child_whole.reshape(panel_width, child_blocks, BLOCK_ROWS),
        one_hot(sub_row, child_blocks),
        preferred_element_type=jnp.float32,
    ).astype(jnp.bfloat16)
    leaf_solution = pick_piece(
        leaf_full.reshape(panel_width, n_col, sub_size * n_row, upd_piece), sub_rank, 2
    )
    return (solution_root, solution_child, leaf_solution)


def solution(mesh):
    in_specs = (
        P("col", None, ("leaf", "row")),
        P("col", None, ("leaf", "row")),
        P("col", None, ("leaf", "row")),
        P(None, ("leaf", "row"), "col"),
        P(None, ("leaf", "row"), "col"),
        P(None, ("leaf", "row"), "col"),
        P(),
        P(),
    )
    out_specs = (
        P("col", None, ("leaf", "row")),
        P("col", None, ("leaf", "row")),
        P("col", None, ("leaf", "row")),
    )
    return jax.shard_map(local, mesh=mesh, in_specs=in_specs, out_specs=out_specs, check_vma=False)
```

profile of v0, /device:TPU:0, one launch (start us, length us, event | category | flops | bytes accessed | tf_op | source)
XLA Modules:
  0.0 315.4 jit_solution(6186895764628182573)
XLA Ops:
  7.2 0.9 copy.131
  9.2 9.2 %all_gather.21 = bf16[16,4,448]{0,1,2:T(4,128)(2,1)S(1)} all-gather(bf16[16,4,224]{0,1,2:T(4,128)(2,1)S(1)} %pad_maximum_fusion), channel_id=1, replica_groups=mesh['leaf'=4,'row'=2,'col'=4] {'row'}, dimensions={2}, use_global_device_ids=true | all-gather | bytes 86016 | tf_op jit(solution)/shard_map/all_gather | solution.py:20
  18.4 1.8 collective-permute-start
  20.6 9.6 %collective-permute-done = bf16[16,4,448]{0,1,2:T(4,128)(2,1)S(1)} collective-permute-done((bf16[16,4,448]{0,1,2:T(4,128)(2,1)S(1)}, bf16[16,4,448]{0,1,2:T(4,128)(2,1)S(1)}, u32[]{:S(2)}, u32[]{:S(2)}) %collective-permute-start) | collective-permute-done | bytes 57376 | tf_op jit(solution)/shard_map/ppermute | solution.py:16
  32.2 3.3 %all-to-all-start = ((bf16[16,4,384]{2,0,1:T(8,128)(2,1)}), bf16[16,4,384]{2,0,1:T(8,128)(2,1)S(1)}, u32[]{:S(2)}, u32[]{:S(2)}) async-start(bf16[16,4,384]{2,0,1:T(8,128)(2,1)} %bitcast.141), calls=%async_computation | async-start | bytes 98304 | tf_op jit(solution)/shard_map/all_to_all | solution.py:114
  35.5 3.9 %all-to-all-done = bf16[16,4,384]{2,0,1:T(8,128)(2,1)S(1)} async-done(((bf16[16,4,384]{2,0,1:T(8,128)(2,1)}), bf16[16,4,384]{2,0,1:T(8,128)(2,1)S(1)}, u32[]{:S(2)}, u32[]{:S(2)}) %all-to-all-start) | async-done | bytes 49184 | tf_op jit(solution)/shard_map/all_to_all | solution.py:114
  39.7 11.1 %psum.14 = bf16[64,384]{1,0:T(8,128)(2,1)S(1)} all-reduce(f32[64,384]{1,0:T(8,128)S(1)} %fusion.31), channel_id=1, replica_groups=mesh['leaf'=4,'row'=2,'col'=4] {'col'}, use_global_device_ids=true, to_apply=%region_0.1 | all-reduce | flops 24576 | bytes 147456 | tf_op jit(solution)/shard_map/psum | solution.py:121
  51.1 4.8 %all_gather.22 = bf16[64,1,192]{0,1,2:T(2,128)(2,1)S(1)} all-gather(bf16[64,1,96]{0,1,2:T(2,128)(2,1)S(1)} %copy.178), channel_id=1, replica_groups=mesh['leaf'=4,'row'=2,'col'=4] {'row'}, dimensions={2}, use_global_device_ids=true | all-gather | bytes 36864 | tf_op jit(solution)/shard_map/all_gather | solution.py:20
  55.9 1.6 collective-permute-start.1
  57.5 2.4 collective-permute-done.1
  61.4 20.5 %reduce-scatter.11.cloned.1.call-done = f32[16,512]{1,0:T(8,128)} async-done(((f32[64,512]{1,0:T(8,128)}), f32[16,512]{1,0:T(8,128)}) %reduce-scatter.11.cloned.1.call-update) | async-done | bytes 32784 | tf_op jit(solution)/shard_map/reduce_scatter | solution.py:126
  83.1 41.1 %all_gather.23 = bf16[16,4,1792]{0,1,2:T(4,128)(2,1)S(1)} all-gather(bf16[16,4,224]{0,1,2:T(4,128)(2,1)S(1)} %pad_maximum_fusion.1), channel_id=1, replica_groups=mesh['leaf'=4,'row'=2,'col'=4] {'leaf','row'}, dimensions={2}, use_global_device_ids=true | all-gather | bytes 258048 | tf_op jit(solution)/shard_map/all_gather | solution.py:134
  126.7 6.7 %all_to_all.66 = bf16[16,4,768]{2,0,1:T(8,128)(2,1)S(1)} all-to-all(bf16[16,4,768]{2,0,1:T(8,128)(2,1)S(1)} %fusion.1), channel_id=1, replica_groups=mesh['leaf'=4,'row'=2,'col'=4] {'col'}, dimensions={1} | all-to-all | bytes 196608 | tf_op jit(solution)/shard_map/all_to_all | solution.py:151
  133.7 11.2 %psum.15 = bf16[64,384]{1,0:T(8,128)(2,1)S(1)} all-reduce(f32[64,384]{1,0:T(8,128)S(1)} %fusion.32), channel_id=1, replica_groups=mesh['leaf'=4,'row'=2,'col'=4] {'col'}, use_global_device_ids=true, to_apply=%region_2.3 | all-reduce | flops 24576 | bytes 147456 | tf_op jit(solution)/shard_map/psum | solution.py:158
  145.0 0.9 copy.172
  146.0 60.1 %reduce-scatter.13.cloned.1.call-done = f32[96,64]{1,0:T(8,128)} async-done(((f32[768,64]{1,0:T(8,128)}), f32[96,64]{1,0:T(8,128)}) %reduce-scatter.13.cloned.1.call-update) | async-done | bytes 24592
  206.1 1.5 copy.173
  207.6 3.3 %all-to-all-start.2 = ((f32[64,1,96]{2,1,0:T(1,128)}), f32[64,1,96]{2,1,0:T(1,128)S(1)}, u32[]{:S(2)}, u32[]{:S(2)}) async-start(f32[64,1,96]{2,1,0:T(1,128)} %bitcast.28), calls=%async_computation.3 | async-start | bytes 65536 | tf_op jit(solution)/shard_map/all_to_all | solution.py:163
  211.0 3.8 %all-to-all-done.2 = f32[64,1,96]{2,1,0:T(1,128)S(1)} async-done(((f32[64,1,96]{2,1,0:T(1,128)}), f32[64,1,96]{2,1,0:T(1,128)S(1)}, u32[]{:S(2)}, u32[]{:S(2)}) %all-to-all-start.2) | async-done | bytes 24608 | tf_op jit(solution)/shard_map/all_to_all | solution.py:163
  215.0 32.0 %all_gather.24 = bf16[16,4,768]{0,1,2:T(4,128)(2,1)S(1)} all-gather(bf16[16,4,96]{0,1,2:T(4,128)(2,1)S(1)} %bitcast.161), channel_id=1, replica_groups=mesh['leaf'=4,'row'=2,'col'=4] {'leaf','row'}, dimensions={2}, use_global_device_ids=true | all-gather | bytes 110592 | tf_op jit(solution)/shard_map/all_gather | solution.py:170
  247.8 5.2 %all-gather = bf16[64,4,1,128]{3,0,1,2:T(8,128)(2,1)S(1)} all-gather(bf16[16,4,1,128]{3,0,1,2:T(8,128)(2,1)S(1)} %copy.181), channel_id=2, replica_groups=mesh['leaf'=4,'row'=2,'col'=4] {'col'}, dimensions={0}, use_global_device_ids=true | all-gather | bytes 81920 | tf_op jit(solution)/shard_map/all_gather | solution.py:186
  253.4 3.9 %collective-permute-done.2 = bf16[64,192]{1,0:T(8,128)(2,1)S(1)} collective-permute-done((bf16[64,192]{1,0:T(8,128)(2,1)S(1)}, bf16[64,192]{1,0:T(8,128)(2,1)S(1)}, u32[]{:S(2)}, u32[]{:S(2)}) %collective-permute-start.2) | collective-permute-done | bytes 24608 | tf_op jit(solution)/shard_map/ppermute | solution.py:16
  258.3 8.1 %reduce-scatter.15.cloned.1.call-done = bf16[96,64]{1,0:T(8,128)(2,1)} async-done(((bf16[192,64]{1,0:T(8,128)(2,1)}), bf16[96,64]{1,0:T(8,128)(2,1)}) %reduce-scatter.15.cloned.1.call-update) | async-done | bytes 12304
  267.2 5.2 %all-gather.2 = bf16[4,96,64]{1,2,0:T(8,128)(2,1)S(1)} all-gather(bf16[1,96,64]{1,2,0:T(8,128)(2,1)S(1)} %copy.154), channel_id=3, replica_groups=mesh['leaf'=4,'row'=2,'col'=4] {'col'}, dimensions={0}, use_global_device_ids=true | all-gather | bytes 61440 | tf_op jit(solution)/shard_map/all_gather | solution.py:193
  273.1 1.6 collective-permute-start.3
  274.6 2.4 collective-permute-done.3
  277.9 10.0 %reduce-scatter.17.cloned.1.call-done = bf16[96,64]{1,0:T(8,128)(2,1)} async-done(((bf16[192,64]{1,0:T(8,128)(2,1)}), bf16[96,64]{1,0:T(8,128)(2,1)}) %reduce-scatter.17.cloned.1.call-update) | async-done | bytes 12304
  289.3 3.3 %all-to-all-start.3 = ((f32[64,1,96]{2,1,0:T(1,128)}), f32[64,1,96]{2,1,0:T(1,128)S(1)}, u32[]{:S(2)}, u32[]{:S(2)}) async-start(f32[64,1,96]{2,1,0:T(1,128)} %bitcast.46), calls=%async_computation.4 | async-start | bytes 65536 | tf_op jit(solution)/shard_map/all_to_all | solution.py:197
  292.6 3.9 %all-to-all-done.3 = f32[64,1,96]{2,1,0:T(1,128)S(1)} async-done(((f32[64,1,96]{2,1,0:T(1,128)}), f32[64,1,96]{2,1,0:T(1,128)S(1)}, u32[]{:S(2)}, u32[]{:S(2)}) %all-to-all-start.3) | async-done | bytes 24608 | tf_op jit(solution)/shard_map/all_to_all | solution.py:197
  296.7 5.3 %all_gather.27 = bf16[16,4,192]{0,1,2:T(4,128)(2,1)S(1)} all-gather(bf16[16,4,96]{0,1,2:T(4,128)(2,1)S(1)} %bitcast.162), channel_id=1, replica_groups=mesh['leaf'=4,'row'=2,'col'=4] {'row'}, dimensions={2}, use_global_device_ids=true | all-gather | bytes 36864 | tf_op jit(solution)/shard_map/all_gather | solution.py:20
  302.0 1.5 collective-permute-start.4
  304.9 2.8 collective-permute-done.4
  (102 shorter events, 18.1 us)
Async XLA Ops:
  7.2 126.2 %copy-start = (bf16[4,96,768]{2,1,0:T(8,128)(2,1)S(1)}, bf16[4,96,768]{2,1,0:T(8,128)(2,1)}, u32[]{:S(2)}) copy-start(bf16[4,96,768]{2,1,0:T(8,128)(2,1)} %param.11) | copy-start | bytes 1769476
  7.2 13.4 %copy-start.5 = (s32[4,8]{1,0:T(4,128)S(1)}, s32[4,8]{1,0:T(4,128)}, u32[]{:S(2)}) copy-start(s32[4,8]{1,0:T(4,128)} %param.15) | copy-start | bytes 388
  18.4 21.0 %copy-start.2 = (bf16[4,96,384]{2,1,0:T(8,128)(2,1)S(1)}, bf16[4,96,384]{2,1,0:T(8,128)(2,1)}, u32[]{:S(2)}) copy-start(bf16[4,96,384]{2,1,0:T(8,128)(2,1)} %param.12) | copy-start | bytes 884740
  18.4 11.7 %collective-permute-start = (bf16[16,4,448]{0,1,2:T(4,128)(2,1)S(1)}, bf16[16,4,448]{0,1,2:T(4,128)(2,1)S(1)}, u32[]{:S(2)}, u32[]{:S(2)}) collective-permute-start(bf16[16,4,448]{0,1,2:T(4,128)(2,1)S(1)} %all_gather.21), channel_id=1, source_target_pairs={{0,8},{8,0},{16,24},{24,16},{1,9},{9,1},{17,25},{25,17},{2,10},{10... | collective-permute-start | bytes 172040 | tf_op jit(solution)/shard_map/ppermute | solution.py:16
  30.4 29.5 %copy-start.1 = (bf16[4,128,384]{2,1,0:T(8,128)(2,1)S(1)}, bf16[4,128,384]{2,1,0:T(8,128)(2,1)}, u32[]{:S(2)}) copy-start(bf16[4,128,384]{2,1,0:T(8,128)(2,1)} %param.13) | copy-start | bytes 1179652
  30.9 30.0 %copy-start.3 = (bf16[16,4,96]{2,1,0:T(4,128)(2,1)S(1)}, bf16[16,4,96]{2,1,0:T(4,128)(2,1)}, u32[]{:S(2)}) copy-start(bf16[16,4,96]{2,1,0:T(4,128)(2,1)} %param.8) | copy-start | bytes 36868
  32.2 7.3 %all-to-all-start = ((bf16[16,4,384]{2,0,1:T(8,128)(2,1)}), bf16[16,4,384]{2,0,1:T(8,128)(2,1)S(1)}, u32[]{:S(2)}, u32[]{:S(2)}) async-start(bf16[16,4,384]{2,0,1:T(8,128)(2,1)} %bitcast.141), calls=%async_computation | async-start | bytes 98304 | tf_op jit(solution)/shard_map/all_to_all | solution.py:114
  35.4 46.4 %reduce-scatter.11.cloned.1.call-start = ((), (), s32[]{:S(2)}) async-start(), calls=%async_computation.8 | async-start | bytes 163840 | tf_op jit(solution)/shard_map/reduce_scatter | solution.py:126
  55.9 4.0 %collective-permute-start.1 = (bf16[64,1,192]{2,0,1:T(8,128)(2,1)S(1)}, bf16[64,1,192]{2,0,1:T(8,128)(2,1)S(1)}, u32[]{:S(2)}, u32[]{:S(2)}) collective-permute-start(bf16[64,1,192]{2,0,1:T(8,128)(2,1)S(1)} %copy.141), channel_id=1, source_target_pairs={{0,8},{8,0},{16,24},{24,16},{1,9},{9,1},{17,25},{25,17},{2,10},{10... | collective-permute-start | bytes 73736 | tf_op jit(solution)/shard_map/ppermute | solution.py:16
  60.8 145.3 %reduce-scatter.13.cloned.1.call-start = ((), (), s32[]{:S(2)}) async-start(), calls=%async_computation.9 | async-start | bytes 442368
  124.5 1.1 copy-start.4
  207.6 7.2 %all-to-all-start.2 = ((f32[64,1,96]{2,1,0:T(1,128)}), f32[64,1,96]{2,1,0:T(1,128)S(1)}, u32[]{:S(2)}, u32[]{:S(2)}) async-start(f32[64,1,96]{2,1,0:T(1,128)} %bitcast.28), calls=%async_computation.3 | async-start | bytes 65536 | tf_op jit(solution)/shard_map/all_to_all | solution.py:163
  210.9 55.5 %reduce-scatter.15.cloned.1.call-start = ((), (), s32[]{:S(2)}) async-start(), calls=%async_computation.10 | async-start | bytes 73728
  253.4 4.0 %collective-permute-start.2 = (bf16[64,192]{1,0:T(8,128)(2,1)S(1)}, bf16[64,192]{1,0:T(8,128)(2,1)S(1)}, u32[]{:S(2)}, u32[]{:S(2)}) collective-permute-start(bf16[64,192]{1,0:T(8,128)(2,1)S(1)} %select_convert_fusion.1), channel_id=1, source_target_pairs={{0,8},{8,0},{16,24},{24,16},{1,9},{9,1},{17,25},{25,17},{2,10},{10... | collective-permute-start | bytes 73736 | tf_op jit(solution)/shard_map/ppermute | solution.py:16
  258.2 29.7 %reduce-scatter.17.cloned.1.call-start = ((), (), s32[]{:S(2)}) async-start(), calls=%async_computation.11 | async-start | bytes 73728
  273.1 4.0 %collective-permute-start.3 = (bf16[64,192]{1,0:T(8,128)(2,1)S(1)}, bf16[64,192]{1,0:T(8,128)(2,1)S(1)}, u32[]{:S(2)}, u32[]{:S(2)}) collective-permute-start(bf16[64,192]{1,0:T(8,128)(2,1)S(1)} %select_convert_fusion), channel_id=1, source_target_pairs={{0,8},{8,0},{16,24},{24,16},{1,9},{9,1},{17,25},{25,17},{2,10},{10... | collective-permute-start | bytes 73736 | tf_op jit(solution)/shard_map/ppermute | solution.py:16
  289.3 7.2 %all-to-all-start.3 = ((f32[64,1,96]{2,1,0:T(1,128)}), f32[64,1,96]{2,1,0:T(1,128)S(1)}, u32[]{:S(2)}, u32[]{:S(2)}) async-start(f32[64,1,96]{2,1,0:T(1,128)} %bitcast.46), calls=%async_computation.4 | async-start | bytes 65536 | tf_op jit(solution)/shard_map/all_to_all | solution.py:197
  302.0 5.7 %collective-permute-start.4 = (bf16[16,4,192]{0,1,2:T(4,128)(2,1)S(1)}, bf16[16,4,192]{0,1,2:T(4,128)(2,1)S(1)}, u32[]{:S(2)}, u32[]{:S(2)}) collective-permute-start(bf16[16,4,192]{0,1,2:T(4,128)(2,1)S(1)} %all_gather.27), channel_id=1, source_target_pairs={{0,8},{8,0},{16,24},{24,16},{1,9},{9,1},{17,25},{25,17},{2,10},{10... | collective-permute-start | bytes 73736 | tf_op jit(solution)/shard_map/ppermute | solution.py:16
Sparse Core Ops, SparseCore 0:
  60.9 20.8 reduce-scatter.10
  146.1 59.9 reduce-scatter.12
  258.3 8.0 reduce-scatter.14
  278.0 9.8 reduce-scatter.16
where the time goes:
time: 316 us; the launch traced here: 315 us
  blocking collectives  132 us (42%)
  waiting for transfers between devices  132 us (42%)
  starting transfers between devices  16.5 us (5%)
  local copies, waits for them, and re-layouts  15.4 us (5%)
  between operations  14.4 us (5%)
    unnamed x7, waiting for transfers between devices  78.3 us
    all_gather x1, blocking collectives, local(): lax.all_gather(joined_root, ('leaf', 'row'), axis=2, tiled=True)  41.1 us
    all_gather x1, blocking collectives, local(): lax.all_gather(solution_root.astype(jnp.bfloat16), ('leaf', 'row'), axis=...  32 us
    ppermute x5, waiting for transfers between devices, partner_2(): return lax.ppermute(block, axis, route)  21.1 us
    reduce_scatter x1, waiting for transfers between devices, local(): lax.psum_scatter(contract(forward_tile, off_matrix, 1, 1), 'col', scatter...  20.5 us
    all_gather x3, blocking collectives, group_gather(): merged = lax.all_gather(piece, 'row', axis=2, tiled=True)  19.3 us
    psum x1, blocking collectives, local(): lax.psum(contract(root_tile, root_matrix, 1, 1), 'col').astype(jnp.bfloat16)  11.2 us
    psum x1, blocking collectives, local(): lax.psum(contract(child_tile, child_matrix, 1, 1), 'col')  11.1 us
  transfers between devices with their start and end apart: 12, of which 12 were waited for; matrix products, arithmetic and copies ran while one was open for 1% of the time, Pallas kernels for 0%

commit v1 on v0

--- a/solution.py
+++ b/solution.py
@@ -4,6 +4,28 @@
 from jax.sharding import PartitionSpec as P
 
 BLOCK_ROWS = 128
+
+
+def joined_along(tiles, dim):
+    shape = list(tiles.shape[1:])
+    shape[dim] *= tiles.shape[0]
+    return jnp.moveaxis(tiles, 0, dim).reshape(shape)
+
+
+def collect(x, axis, dim):
+    size = lax.axis_size(axis)
+    pairs = [(i, (i + 1) % size) for i in range(size)]
+    back = [(b, a) for a, b in pairs]
+    lower, upper = ([], [])
+    for lap in range(size - 1):
+        if lap % 2 == 0:
+            lower.append(lax.ppermute(lower[-1] if lower else x, axis, pairs))
+        else:
+            upper.append(lax.ppermute(upper[-1] if upper else x, axis, back))
+    tiles = jnp.stack([*lower[::-1], x, *upper])
+    shift = lax.axis_index(axis) - len(lower)
+    tiles = tiles[(jnp.arange(size) - shift) % size]
+    return joined_along(tiles, dim)
 
 
 def partner_2(block, axis, bit):
@@ -131,7 +153,7 @@
     )
     child_pass = (tail_mine - pass_term.reshape(panel_width, n_col, upd_piece)).astype(jnp.bfloat16)
     joined_root = jnp.concatenate([child_pass, rhs_root], 2)
-    root_all = lax.all_gather(joined_root, ("leaf", "row"), axis=2, tiled=True).reshape(
+    root_all = collect(joined_root, ("leaf", "row"), 2).reshape(
         panel_width, n_col, n_leaf * n_row, upd_piece + sep_piece
     )
     pass_vectors = (

time: 316 us -> 303 us (0.959)
  blocking collectives: 132 us -> 90.9 us
  starting transfers between devices: 16.5 us -> 32.2 us
  waiting for transfers between devices: 132 us -> 144 us
    all_gather x1 -> x0, blocking collectives: 41.1 us -> none  [local(): lax.all_gather(joined_root, ('leaf', 'row'), axis=2, tiled=True)]
    ppermute x0 -> x7, starting transfers between devices: none -> 15.8 us  [the longest x3 14.3 us: collect(): upper.append(lax.ppermute(upper[-1] if upper else x, axis, back))]
    ppermute x0 -> x7, waiting for transfers between devices: none -> 10.7 us  [the longest x4 10.7 us: collect(): lower.append(lax.ppermute(lower[-1] if lower else x, axis, pairs))]
    unnamed x29 -> x36, local copies, waits for them, and re-layouts: 8.16 us -> 8.81 us
  transfers between devices with their start and end apart: 12 -> 19, of which waited for: 12 -> 16; matrix products, arithmetic and copies ran while one was open for 1% -> 1% of each run, Pallas kernels for 0% -> 0%
where the time goes in v1:
time: 303 us; the launch traced here: 302 us
  waiting for transfers between devices  144 us (48%)
  blocking collectives  90.9 us (30%)
  starting transfers between devices  32.2 us (11%)
  local copies, waits for them, and re-layouts  14.5 us (5%)
  between operations  14.4 us (5%)
  other arithmetic  3.24 us (1%)
  matrix products  3.06 us (1%)
    unnamed x7, waiting for transfers between devices  80.9 us
    all_gather x1, blocking collectives, local(): lax.all_gather(solution_root.astype(jnp.bfloat16), ('leaf', 'row'), axis=...  32 us
    ppermute x5, waiting for transfers between devices, partner_2(): return lax.ppermute(block, axis, route)  20.4 us
    reduce_scatter x1, waiting for transfers between devices, local(): lax.psum_scatter(contract(forward_tile, off_matrix, 1, 1), 'col', scatter...  20.1 us
    all_gather x3, blocking collectives, group_gather(): merged = lax.all_gather(piece, 'row', axis=2, tiled=True)  19.3 us
    ppermute x3, starting transfers between devices, collect(): upper.append(lax.ppermute(upper[-1] if upper else x, axis, back))  14.3 us
    psum x1, blocking collectives, local(): lax.psum(contract(child_tile, child_matrix, 1, 1), 'col')  11.2 us
    psum x1, blocking collectives, local(): lax.psum(contract(root_tile, root_matrix, 1, 1), 'col').astype(jnp.bfloat16)  11.2 us
  transfers between devices with their start and end apart: 19, of which 16 were waited for; matrix products, arithmetic and copies ran while one was open for 1% of the time, Pallas kernels for 0%

profile of v1, /device:TPU:0, one launch (start us, length us, event | category | flops | bytes accessed | tf_op | source)
XLA Modules:
  0.0 302.2 jit_solution(2397453470698376762)
XLA Ops:
  8.5 9.2 %all_gather.18 = bf16[16,4,448]{0,1,2:T(4,128)(2,1)S(1)} all-gather(bf16[16,4,224]{0,1,2:T(4,128)(2,1)S(1)} %pad_maximum_fusion), channel_id=1, replica_groups=mesh['leaf'=4,'row'=2,'col'=4] {'row'}, dimensions={2}, use_global_device_ids=true | all-gather | bytes 86016 | tf_op jit(solution)/shard_map/all_gather | solution.py:42
  17.7 1.8 collective-permute-start
  20.5 8.9 %collective-permute-done = bf16[16,4,448]{0,1,2:T(4,128)(2,1)S(1)} collective-permute-done((bf16[16,4,448]{0,1,2:T(4,128)(2,1)S(1)}, bf16[16,4,448]{0,1,2:T(4,128)(2,1)S(1)}, u32[]{:S(2)}, u32[]{:S(2)}) %collective-permute-start) | collective-permute-done | bytes 57376 | tf_op jit(solution)/shard_map/ppermute | solution.py:38
  31.4 3.3 %all-to-all-start = ((bf16[16,4,384]{2,0,1:T(8,128)(2,1)}), bf16[16,4,384]{2,0,1:T(8,128)(2,1)S(1)}, u32[]{:S(2)}, u32[]{:S(2)}) async-start(bf16[16,4,384]{2,0,1:T(8,128)(2,1)} %bitcast.167), calls=%async_computation | async-start | bytes 98304 | tf_op jit(solution)/shard_map/all_to_all | solution.py:136
  34.8 3.9 %all-to-all-done = bf16[16,4,384]{2,0,1:T(8,128)(2,1)S(1)} async-done(((bf16[16,4,384]{2,0,1:T(8,128)(2,1)}), bf16[16,4,384]{2,0,1:T(8,128)(2,1)S(1)}, u32[]{:S(2)}, u32[]{:S(2)}) %all-to-all-start) | async-done | bytes 49184 | tf_op jit(solution)/shard_map/all_to_all | solution.py:136
  38.9 11.2 %psum.14 = bf16[64,384]{1,0:T(8,128)(2,1)S(1)} all-reduce(f32[64,384]{1,0:T(8,128)S(1)} %fusion.33), channel_id=1, replica_groups=mesh['leaf'=4,'row'=2,'col'=4] {'col'}, use_global_device_ids=true, to_apply=%region_0.1 | all-reduce | flops 24576 | bytes 147456 | tf_op jit(solution)/shard_map/psum | solution.py:143
  50.5 4.8 %all_gather.19 = bf16[64,1,192]{0,1,2:T(2,128)(2,1)S(1)} all-gather(bf16[64,1,96]{0,1,2:T(2,128)(2,1)S(1)} %copy.195), channel_id=1, replica_groups=mesh['leaf'=4,'row'=2,'col'=4] {'row'}, dimensions={2}, use_global_device_ids=true | all-gather | bytes 36864 | tf_op jit(solution)/shard_map/all_gather | solution.py:42
  56.9 2.4 collective-permute-done.1
  61.1 20.1 %reduce-scatter.11.cloned.1.call-done = f32[16,512]{1,0:T(8,128)} async-done(((f32[64,512]{1,0:T(8,128)}), f32[16,512]{1,0:T(8,128)}) %reduce-scatter.11.cloned.1.call-update) | async-done | bytes 32784 | tf_op jit(solution)/shard_map/reduce_scatter | solution.py:148
  83.6 5.1 %collective-permute-done.2 = bf16[16,4,224]{2,0,1:T(8,128)(2,1)S(1)} collective-permute-done((bf16[16,4,224]{2,0,1:T(8,128)(2,1)S(1)}, bf16[16,4,224]{2,0,1:T(8,128)(2,1)S(1)}, u32[]{:S(2)}, u32[]{:S(2)}) %collective-permute-start.2) | collective-permute-done | bytes 28704 | tf_op jit(solution)/shard_map/ppermute | solution.py:22
  88.7 4.7 %collective-permute-start.6 = (bf16[16,4,224]{2,0,1:T(8,128)(2,1)S(1)}, bf16[16,4,224]{2,0,1:T(8,128)(2,1)S(1)}, u32[]{:S(2)}, u32[]{:S(2)}) collective-permute-start(bf16[16,4,224]{2,0,1:T(8,128)(2,1)S(1)} %pad_maximum_fusion.2), channel_id=1, source_target_pairs={{4,0},{8,4},{12,8},{16,12},{20,16},{24,20},{28,24},{0,28},{5,1},{9... | collective-permute-start | bytes 86024 | tf_op jit(solution)/shard_map/ppermute | solution.py:24
  93.4 1.9 collective-permute-done.3
  95.4 4.8 %collective-permute-start.7 = (bf16[16,4,224]{2,0,1:T(8,128)(2,1)S(1)}, bf16[16,4,224]{2,0,1:T(8,128)(2,1)S(1)}, u32[]{:S(2)}, u32[]{:S(2)}) collective-permute-start(bf16[16,4,224]{2,0,1:T(8,128)(2,1)S(1)} %collective-permute-done.6), channel_id=1, source_target_pairs={{4,0},{8,4},{12,8},{16,12},{20,16},{24,20},{28,24},{0,28},{5,1},{9... | collective-permute-start | bytes 86024 | tf_op jit(solution)/shard_map/ppermute | solution.py:24
  100.1 1.8 collective-permute-done.4
  102.0 4.8 %collective-permute-start.8 = (bf16[16,4,224]{2,0,1:T(8,128)(2,1)S(1)}, bf16[16,4,224]{2,0,1:T(8,128)(2,1)S(1)}, u32[]{:S(2)}, u32[]{:S(2)}) collective-permute-start(bf16[16,4,224]{2,0,1:T(8,128)(2,1)S(1)} %collective-permute-done.7), channel_id=1, source_target_pairs={{4,0},{8,4},{12,8},{16,12},{20,16},{24,20},{28,24},{0,28},{5,1},{9... | collective-permute-start | bytes 86024 | tf_op jit(solution)/shard_map/ppermute | solution.py:24
  106.8 1.8 collective-permute-done.5
  110.9 6.7 %all_to_all.66 = bf16[16,4,768]{2,0,1:T(8,128)(2,1)S(1)} all-to-all(bf16[16,4,768]{2,0,1:T(8,128)(2,1)S(1)} %fusion), channel_id=1, replica_groups=mesh['leaf'=4,'row'=2,'col'=4] {'col'}, dimensions={1} | all-to-all | bytes 196608 | tf_op jit(solution)/shard_map/all_to_all | solution.py:173
  117.9 11.2 %psum.15 = bf16[64,384]{1,0:T(8,128)(2,1)S(1)} all-reduce(f32[64,384]{1,0:T(8,128)S(1)} %fusion.34), channel_id=1, replica_groups=mesh['leaf'=4,'row'=2,'col'=4] {'col'}, use_global_device_ids=true, to_apply=%region_2.3 | all-reduce | flops 24576 | bytes 147456 | tf_op jit(solution)/shard_map/psum | solution.py:180
  130.2 62.7 %reduce-scatter.13.cloned.1.call-done = f32[96,64]{1,0:T(8,128)} async-done(((f32[768,64]{1,0:T(8,128)}), f32[96,64]{1,0:T(8,128)}) %reduce-scatter.13.cloned.1.call-update) | async-done | bytes 24592
  194.4 3.3 %all-to-all-start.2 = ((f32[64,1,96]{2,1,0:T(1,128)}), f32[64,1,96]{2,1,0:T(1,128)S(1)}, u32[]{:S(2)}, u32[]{:S(2)}) async-start(f32[64,1,96]{2,1,0:T(1,128)} %bitcast.37), calls=%async_computation.3 | async-start | bytes 65536 | tf_op jit(solution)/shard_map/all_to_all | solution.py:185
  197.8 3.8 %all-to-all-done.2 = f32[64,1,96]{2,1,0:T(1,128)S(1)} async-done(((f32[64,1,96]{2,1,0:T(1,128)}), f32[64,1,96]{2,1,0:T(1,128)S(1)}, u32[]{:S(2)}, u32[]{:S(2)}) %all-to-all-start.2) | async-done | bytes 24608 | tf_op jit(solution)/shard_map/all_to_all | solution.py:185
  201.8 32.0 %all_gather.20 = bf16[16,4,768]{0,1,2:T(4,128)(2,1)S(1)} all-gather(bf16[16,4,96]{0,1,2:T(4,128)(2,1)S(1)} %bitcast.186), channel_id=1, replica_groups=mesh['leaf'=4,'row'=2,'col'=4] {'leaf','row'}, dimensions={2}, use_global_device_ids=true | all-gather | bytes 110592 | tf_op jit(solution)/shard_map/all_gather | solution.py:192
  234.6 5.2 %all-gather = bf16[64,4,1,128]{3,0,1,2:T(8,128)(2,1)S(1)} all-gather(bf16[16,4,1,128]{3,0,1,2:T(8,128)(2,1)S(1)} %copy.196), channel_id=2, replica_groups=mesh['leaf'=4,'row'=2,'col'=4] {'col'}, dimensions={0}, use_global_device_ids=true | all-gather | bytes 81920 | tf_op jit(solution)/shard_map/all_gather | solution.py:208
  240.3 3.9 %collective-permute-done.9 = bf16[64,192]{1,0:T(8,128)(2,1)S(1)} collective-permute-done((bf16[64,192]{1,0:T(8,128)(2,1)S(1)}, bf16[64,192]{1,0:T(8,128)(2,1)S(1)}, u32[]{:S(2)}, u32[]{:S(2)}) %collective-permute-start.9) | collective-permute-done | bytes 24608 | tf_op jit(solution)/shard_map/ppermute | solution.py:38
  245.1 8.1 %reduce-scatter.15.cloned.1.call-done = bf16[96,64]{1,0:T(8,128)(2,1)} async-done(((bf16[192,64]{1,0:T(8,128)(2,1)}), bf16[96,64]{1,0:T(8,128)(2,1)}) %reduce-scatter.15.cloned.1.call-update) | async-done | bytes 12304
  254.0 5.2 %all-gather.2 = bf16[4,96,64]{1,2,0:T(8,128)(2,1)S(1)} all-gather(bf16[1,96,64]{1,2,0:T(8,128)(2,1)S(1)} %copy.170), channel_id=3, replica_groups=mesh['leaf'=4,'row'=2,'col'=4] {'col'}, dimensions={0}, use_global_device_ids=true | all-gather | bytes 61440 | tf_op jit(solution)/shard_map/all_gather | solution.py:215
  261.4 2.4 collective-permute-done.10
  264.7 10.0 %reduce-scatter.17.cloned.1.call-done = bf16[96,64]{1,0:T(8,128)(2,1)} async-done(((bf16[192,64]{1,0:T(8,128)(2,1)}), bf16[96,64]{1,0:T(8,128)(2,1)}) %reduce-scatter.17.cloned.1.call-update) | async-done | bytes 12304
  276.2 3.3 %all-to-all-start.3 = ((f32[64,1,96]{2,1,0:T(1,128)}), f32[64,1,96]{2,1,0:T(1,128)S(1)}, u32[]{:S(2)}, u32[]{:S(2)}) async-start(f32[64,1,96]{2,1,0:T(1,128)} %bitcast.55), calls=%async_computation.4 | async-start | bytes 65536 | tf_op jit(solution)/shard_map/all_to_all | solution.py:219
  279.4 3.9 %all-to-all-done.3 = f32[64,1,96]{2,1,0:T(1,128)S(1)} async-done(((f32[64,1,96]{2,1,0:T(1,128)}), f32[64,1,96]{2,1,0:T(1,128)S(1)}, u32[]{:S(2)}, u32[]{:S(2)}) %all-to-all-start.3) | async-done | bytes 24608 | tf_op jit(solution)/shard_map/all_to_all | solution.py:219
  283.5 5.3 %all_gather.23 = bf16[16,4,192]{0,1,2:T(4,128)(2,1)S(1)} all-gather(bf16[16,4,96]{0,1,2:T(4,128)(2,1)S(1)} %bitcast.187), channel_id=1, replica_groups=mesh['leaf'=4,'row'=2,'col'=4] {'row'}, dimensions={2}, use_global_device_ids=true | all-gather | bytes 36864 | tf_op jit(solution)/shard_map/all_gather | solution.py:42
  291.7 2.8 collective-permute-done.11
  (126 shorter events, 27.3 us)
Async XLA Ops:
  7.2 110.4 %copy-start = (bf16[4,96,768]{2,1,0:T(8,128)(2,1)S(1)}, bf16[4,96,768]{2,1,0:T(8,128)(2,1)}, u32[]{:S(2)}) copy-start(bf16[4,96,768]{2,1,0:T(8,128)(2,1)} %param.11) | copy-start | bytes 1769476
  7.2 1.0 copy-start.3
  17.7 11.7 %collective-permute-start = (bf16[16,4,448]{0,1,2:T(4,128)(2,1)S(1)}, bf16[16,4,448]{0,1,2:T(4,128)(2,1)S(1)}, u32[]{:S(2)}, u32[]{:S(2)}) collective-permute-start(bf16[16,4,448]{0,1,2:T(4,128)(2,1)S(1)} %all_gather.18), channel_id=1, source_target_pairs={{0,8},{8,0},{16,24},{24,16},{1,9},{9,1},{17,25},{25,17},{2,10},{10... | collective-permute-start | bytes 172040 | tf_op jit(solution)/shard_map/ppermute | solution.py:38
  19.8 0.7 copy-start.6
  30.6 8.1 %copy-start.2 = (bf16[4,96,384]{2,1,0:T(8,128)(2,1)S(1)}, bf16[4,96,384]{2,1,0:T(8,128)(2,1)}, u32[]{:S(2)}) copy-start(bf16[4,96,384]{2,1,0:T(8,128)(2,1)} %param.12) | copy-start | bytes 884740
  31.4 7.3 %all-to-all-start = ((bf16[16,4,384]{2,0,1:T(8,128)(2,1)}), bf16[16,4,384]{2,0,1:T(8,128)(2,1)S(1)}, u32[]{:S(2)}, u32[]{:S(2)}) async-start(bf16[16,4,384]{2,0,1:T(8,128)(2,1)} %bitcast.167), calls=%async_computation | async-start | bytes 98304 | tf_op jit(solution)/shard_map/all_to_all | solution.py:136
  34.7 46.6 %reduce-scatter.11.cloned.1.call-start = ((), (), s32[]{:S(2)}) async-start(), calls=%async_computation.8 | async-start | bytes 163840 | tf_op jit(solution)/shard_map/reduce_scatter | solution.py:148
  38.9 20.4 %copy-start.1 = (bf16[4,128,384]{2,1,0:T(8,128)(2,1)S(1)}, bf16[4,128,384]{2,1,0:T(8,128)(2,1)}, u32[]{:S(2)}) copy-start(bf16[4,128,384]{2,1,0:T(8,128)(2,1)} %param.13) | copy-start | bytes 1179652
  55.3 4.0 %collective-permute-start.1 = (bf16[64,1,192]{2,0,1:T(8,128)(2,1)S(1)}, bf16[64,1,192]{2,0,1:T(8,128)(2,1)S(1)}, u32[]{:S(2)}, u32[]{:S(2)}) collective-permute-start(bf16[64,1,192]{2,0,1:T(8,128)(2,1)S(1)} %copy.157), channel_id=1, source_target_pairs={{0,8},{8,0},{16,24},{24,16},{1,9},{9,1},{17,25},{25,17},{2,10},{10... | collective-permute-start | bytes 73736 | tf_op jit(solution)/shard_map/ppermute | solution.py:38
  60.2 0.7 copy-start.4
  60.2 132.7 %reduce-scatter.13.cloned.1.call-start = ((), (), s32[]{:S(2)}) async-start(), calls=%async_computation.9 | async-start | bytes 442368
  82.0 6.7 %collective-permute-start.2 = (bf16[16,4,224]{2,0,1:T(8,128)(2,1)S(1)}, bf16[16,4,224]{2,0,1:T(8,128)(2,1)S(1)}, u32[]{:S(2)}, u32[]{:S(2)}) collective-permute-start(bf16[16,4,224]{2,0,1:T(8,128)(2,1)S(1)} %pad_maximum_fusion.2), channel_id=1, source_target_pairs={{0,4},{4,8},{8,12},{12,16},{16,20},{20,24},{24,28},{28,0},{1,5},{5... | collective-permute-start | bytes 86024 | tf_op jit(solution)/shard_map/ppermute | solution.py:22
  88.7 6.6 %collective-permute-start.3 = (bf16[16,4,224]{2,0,1:T(8,128)(2,1)S(1)}, bf16[16,4,224]{2,0,1:T(8,128)(2,1)S(1)}, u32[]{:S(2)}, u32[]{:S(2)}) collective-permute-start(bf16[16,4,224]{2,0,1:T(8,128)(2,1)S(1)} %collective-permute-done.2), channel_id=1, source_target_pairs={{0,4},{4,8},{8,12},{12,16},{16,20},{20,24},{24,28},{28,0},{1,5},{5... | collective-permute-start | bytes 86024 | tf_op jit(solution)/shard_map/ppermute | solution.py:22
  88.7 6.6 %collective-permute-start.6 = (bf16[16,4,224]{2,0,1:T(8,128)(2,1)S(1)}, bf16[16,4,224]{2,0,1:T(8,128)(2,1)S(1)}, u32[]{:S(2)}, u32[]{:S(2)}) collective-permute-start(bf16[16,4,224]{2,0,1:T(8,128)(2,1)S(1)} %pad_maximum_fusion.2), channel_id=1, source_target_pairs={{4,0},{8,4},{12,8},{16,12},{20,16},{24,20},{28,24},{0,28},{5,1},{9... | collective-permute-start | bytes 86024 | tf_op jit(solution)/shard_map/ppermute | solution.py:24
  95.3 6.6 %collective-permute-start.4 = (bf16[16,4,224]{2,0,1:T(8,128)(2,1)S(1)}, bf16[16,4,224]{2,0,1:T(8,128)(2,1)S(1)}, u32[]{:S(2)}, u32[]{:S(2)}) collective-permute-start(bf16[16,4,224]{2,0,1:T(8,128)(2,1)S(1)} %collective-permute-done.3), channel_id=1, source_target_pairs={{0,4},{4,8},{8,12},{12,16},{16,20},{20,24},{24,28},{28,0},{1,5},{5... | collective-permute-start | bytes 86024 | tf_op jit(solution)/shard_map/ppermute | solution.py:22
  95.4 6.6 %collective-permute-start.7 = (bf16[16,4,224]{2,0,1:T(8,128)(2,1)S(1)}, bf16[16,4,224]{2,0,1:T(8,128)(2,1)S(1)}, u32[]{:S(2)}, u32[]{:S(2)}) collective-permute-start(bf16[16,4,224]{2,0,1:T(8,128)(2,1)S(1)} %collective-permute-done.6), channel_id=1, source_target_pairs={{4,0},{8,4},{12,8},{16,12},{20,16},{24,20},{28,24},{0,28},{5,1},{9... | collective-permute-start | bytes 86024 | tf_op jit(solution)/shard_map/ppermute | solution.py:24
  102.0 6.6 %collective-permute-start.5 = (bf16[16,4,224]{2,0,1:T(8,128)(2,1)S(1)}, bf16[16,4,224]{2,0,1:T(8,128)(2,1)S(1)}, u32[]{:S(2)}, u32[]{:S(2)}) collective-permute-start(bf16[16,4,224]{2,0,1:T(8,128)(2,1)S(1)} %collective-permute-done.4), channel_id=1, source_target_pairs={{0,4},{4,8},{8,12},{12,16},{16,20},{20,24},{24,28},{28,0},{1,5},{5... | collective-permute-start | bytes 86024 | tf_op jit(solution)/shard_map/ppermute | solution.py:22
  102.0 6.7 %collective-permute-start.8 = (bf16[16,4,224]{2,0,1:T(8,128)(2,1)S(1)}, bf16[16,4,224]{2,0,1:T(8,128)(2,1)S(1)}, u32[]{:S(2)}, u32[]{:S(2)}) collective-permute-start(bf16[16,4,224]{2,0,1:T(8,128)(2,1)S(1)} %collective-permute-done.7), channel_id=1, source_target_pairs={{4,0},{8,4},{12,8},{16,12},{20,16},{24,20},{28,24},{0,28},{5,1},{9... | collective-permute-start | bytes 86024 | tf_op jit(solution)/shard_map/ppermute | solution.py:24
  109.5 0.7 copy-start.5
  194.4 7.2 %all-to-all-start.2 = ((f32[64,1,96]{2,1,0:T(1,128)}), f32[64,1,96]{2,1,0:T(1,128)S(1)}, u32[]{:S(2)}, u32[]{:S(2)}) async-start(f32[64,1,96]{2,1,0:T(1,128)} %bitcast.37), calls=%async_computation.3 | async-start | bytes 65536 | tf_op jit(solution)/shard_map/all_to_all | solution.py:185
  197.7 55.5 %reduce-scatter.15.cloned.1.call-start = ((), (), s32[]{:S(2)}) async-start(), calls=%async_computation.10 | async-start | bytes 73728
  240.2 4.0 %collective-permute-start.9 = (bf16[64,192]{1,0:T(8,128)(2,1)S(1)}, bf16[64,192]{1,0:T(8,128)(2,1)S(1)}, u32[]{:S(2)}, u32[]{:S(2)}) collective-permute-start(bf16[64,192]{1,0:T(8,128)(2,1)S(1)} %select_convert_fusion.1), channel_id=1, source_target_pairs={{0,8},{8,0},{16,24},{24,16},{1,9},{9,1},{17,25},{25,17},{2,10},{10... | collective-permute-start | bytes 73736 | tf_op jit(solution)/shard_map/ppermute | solution.py:38
  245.0 29.7 %reduce-scatter.17.cloned.1.call-start = ((), (), s32[]{:S(2)}) async-start(), calls=%async_computation.11 | async-start | bytes 73728
  259.9 4.0 %collective-permute-start.10 = (bf16[64,192]{1,0:T(8,128)(2,1)S(1)}, bf16[64,192]{1,0:T(8,128)(2,1)S(1)}, u32[]{:S(2)}, u32[]{:S(2)}) collective-permute-start(bf16[64,192]{1,0:T(8,128)(2,1)S(1)} %select_convert_fusion), channel_id=1, source_target_pairs={{0,8},{8,0},{16,24},{24,16},{1,9},{9,1},{17,25},{25,17},{2,10},{10... | collective-permute-start | bytes 73736 | tf_op jit(solution)/shard_map/ppermute | solution.py:38
  276.2 7.2 %all-to-all-start.3 = ((f32[64,1,96]{2,1,0:T(1,128)}), f32[64,1,96]{2,1,0:T(1,128)S(1)}, u32[]{:S(2)}, u32[]{:S(2)}) async-start(f32[64,1,96]{2,1,0:T(1,128)} %bitcast.55), calls=%async_computation.4 | async-start | bytes 65536 | tf_op jit(solution)/shard_map/all_to_all | solution.py:219
  288.8 5.7 %collective-permute-start.11 = (bf16[16,4,192]{0,1,2:T(4,128)(2,1)S(1)}, bf16[16,4,192]{0,1,2:T(4,128)(2,1)S(1)}, u32[]{:S(2)}, u32[]{:S(2)}) collective-permute-start(bf16[16,4,192]{0,1,2:T(4,128)(2,1)S(1)} %all_gather.23), channel_id=1, source_target_pairs={{0,8},{8,0},{16,24},{24,16},{1,9},{9,1},{17,25},{25,17},{2,10},{10... | collective-permute-start | bytes 73736 | tf_op jit(solution)/shard_map/ppermute | solution.py:38
Sparse Core Ops, SparseCore 0:
  60.4 20.8 reduce-scatter.10
  130.3 62.5 reduce-scatter.12
  245.1 8.0 reduce-scatter.14
  264.8 9.8 reduce-scatter.16
